TPU v7x, 512 devices: a whole 4x8x8 slice. The times are simulated.
512 devices in a mesh: row: 32 (over x, y), col: 16 (over z, core).
Axes of the slice: x: 4, y: 8, z: 8, core: 2. Of those that a mesh axis runs over, the one named last changes fastest.
Arguments:
- amplitudes: bfloat16 [32768, 32768], P('row', 'col'), may hold values from -6 to 6
- integrals: bfloat16 [32768, 1024], P('col', 'row'), may hold values from -0.03125 to 0.03125
- tile_mask: int32 [256, 256], P('row', 'col'), may hold values 0 or 1
Outputs:
- residual: bfloat16 [32768, 1024], P('row', 'col')
All inputs are finite; a program needn't handle non-finite values. No bound on the sum of `tile_mask` on one device may be relied on, other than what follows from the above.
Results may differ from a plain program's by a relative error of at most 0.001.
Values may be sent and summed in bfloat16 or wider, within the bound.
A program may use at most 64 MiB of HBM per device.

v0:
```python
import jax
import jax.numpy as jnp
from jax import lax
from jax.sharding import PartitionSpec as P


def apply_mask(amplitudes, tile_mask):
    tiles_m, tiles_k = tile_mask.shape
    tile_rows = amplitudes.shape[0] // tiles_m
    tile_cols = amplitudes.shape[1] // tiles_k
    blocks = amplitudes.reshape(tiles_m, tile_rows, tiles_k, tile_cols)
    weights = tile_mask.astype(amplitudes.dtype)[:, None, :, None]
    return (blocks * weights).reshape(amplitudes.shape)


def per_device(amplitudes, integrals, tile_mask):
    masked = apply_mask(amplitudes, tile_mask)
    partial_sums = jnp.dot(
        masked,
        lax.all_gather(integrals, "row", axis=1, tiled=True),
        preferred_element_type=jnp.float32,
    )
    summed = lax.psum_scatter(partial_sums, "col", scatter_dimension=1, tiled=True)
    return summed.astype(jnp.bfloat16)


def solution(mesh):
    placed = (P("row", "col"), P("col", "row"), P("row", "col"))
    return jax.shard_map(
        per_device, mesh=mesh, in_specs=placed, out_specs=P("row", "col"), check_vma=False
    )
```

profile of v0, /device:TPU:2, one launch (start us, length us, event | category | flops | bytes accessed | tf_op | source)
XLA Modules:
  0.0 185.4 jit_solution(4674022924054727534)
XLA Ops:
  6.5 0.0 all-gather.2.cloned.1.call-start
  6.5 0.7 all-gather.2.cloned.1.call-update
  7.3 0.0 reduce-scatter.2.cloned.1.call-start
  7.3 0.7 convert_element_type.6
  8.0 92.9 %all-gather.2.cloned.1.call-done = bf16[2048,1024]{0,1:T(8,128)(2,1)} async-done(((bf16[2048,32]{0,1:T(8,128)(2,1)}), bf16[2048,1024]{0,1:T(8,128)(2,1)}) %all-gather.2.cloned.1.call-update) | async-done | bytes 4194320 | tf_op jit(solution)/shard_map/all_gather | solution.py:20
  100.9 0.0 copy-start
  100.9 0.6 mul.11
  101.5 1.6 copy-done
  103.0 8.5 %fusion = f32[1024,1024]{0,1:T(8,128)} fusion(bf16[2048,1024]{0,1:T(8,128)(2,1)} %all-gather.2.cloned.1.call-done, bf16[1024,2048]{1,0:T(8,128)(2,1)S(1)} %copy-done, bf16[128,8,16,128]{3,2,1,0:T(8,128)(2,1)S(1)} %bitcast.6), kind=kOutput, calls=%fused_computation.1 | convolution fusion | flops 4297064448 | bytes 16777216 | tf_op jit(solution)/shard_map/dot_general | solution.py:18
  111.6 0.0 reduce-scatter.2.cloned.1.call-update
  111.6 65.3 %reduce-scatter.2.cloned.1.call-done = f32[1024,64]{0,1:T(8,128)} async-done(((f32[1024,1024]{0,1:T(8,128)}), f32[1024,64]{0,1:T(8,128)}) %reduce-scatter.2.cloned.1.call-update) | async-done | bytes 262160 | tf_op jit(solution)/shard_map/reduce_scatter | solution.py:23
  176.9 1.6 convert_element_type.7
Async XLA Ops:
  6.5 94.3 %all-gather.2.cloned.1.call-start = ((), (), s32[]{:S(2)}) async-start(), calls=%async_computation.1 | async-start | bytes 4325376 | tf_op jit(solution)/shard_map/all_gather | solution.py:20
  7.3 169.7 %reduce-scatter.2.cloned.1.call-start = ((), (), s32[]{:S(2)}) async-start(), calls=%async_computation.2 | async-start | bytes 4456448 | tf_op jit(solution)/shard_map/reduce_scatter | solution.py:23
  100.9 2.2 %copy-start = (bf16[1024,2048]{1,0:T(8,128)(2,1)S(1)}, bf16[1024,2048]{1,0:T(8,128)(2,1)}, u32[]{:S(2)}) copy-start(bf16[1024,2048]{1,0:T(8,128)(2,1)} %param.3) | copy-start | bytes 12582916
Sparse Core Ops, SparseCore 0:
  10.5 90.2 all-gather.1
  111.7 65.1 reduce-scatter.1
where the time goes:
time: 186 us; the launch traced here: 185 us
  waiting for transfers between devices  159 us (85%)
  between operations  13.4 us (7%)
  matrix products  8.55 us (5%)
  other arithmetic  2.31 us (1%)
  local copies, waits for them, and re-layouts  2.18 us (1%)
    all_gather x1, waiting for transfers between devices, per_device(): lax.all_gather(integrals, 'row', axis=1, tiled=True)  92.9 us
    reduce_scatter x1, waiting for transfers between devices, per_device(): lax.psum_scatter(partial_sums, 'col', scatter_dimension=1, tiled=True)  65.3 us
    dot_general x1, matrix products, per_device(): jnp.dot(masked, lax.all_gather(integrals, 'row', axis=1, tiled=True), pre...  8.55 us
  transfers between devices with their start and end apart: 2, of which 2 were waited for; matrix products, arithmetic and copies ran while one was open for 0% of the time, Pallas kernels for 0%

commit v1 on v0

--- a/solution.py
+++ b/solution.py
@@ -17,7 +17,9 @@
     masked = apply_mask(amplitudes, tile_mask)
     partial_sums = jnp.dot(
         masked,
-        lax.all_gather(integrals, "row", axis=1, tiled=True),
+        jnp.concatenate(
+            lax.all_to_all(jnp.stack([integrals] * lax.axis_size("row")), "row", 0, 0), axis=1
+        ),
         preferred_element_type=jnp.float32,
     )
     summed = lax.psum_scatter(partial_sums, "col", scatter_dimension=1, tiled=True)

time: 186 us -> 203 us (1.091)
  the two profiles are of different devices: /device:TPU:2 before, /device:TPU:8 now
where the time goes in v1:
time: 203 us
  waiting for transfers between devices  163 us (80%)
  between operations  13.4 us (7%)
  starting transfers between devices  10.4 us (5%)
  matrix products  8.57 us (4%)
  local copies, waits for them, and re-layouts  5.57 us (3%)
    all_to_all x1, waiting for transfers between devices, per_device(): lax.all_to_all(jnp.stack([integrals] * lax.axis_size('row')), 'row', 0, 0)  95.1 us
    reduce_scatter x1, waiting for transfers between devices, per_device(): lax.psum_scatter(partial_sums, 'col', scatter_dimension=1, tiled=True)  67.8 us
    all_to_all x1, starting transfers between devices, per_device(): lax.all_to_all(jnp.stack([integrals] * lax.axis_size('row')), 'row', 0, 0)  10.4 us
    dot_general x1, matrix products, per_device(): jnp.dot(masked, jnp.concatenate(lax.all_to_all(jnp.stack([integrals] * la...  8.57 us
  transfers between devices with their start and end apart: 2, of which 2 were waited for; matrix products, arithmetic and copies ran while one was open for 0% of the time, Pallas kernels for 0%

profile of v1, /device:TPU:8, one launch (start us, length us, event | category | flops | bytes accessed | tf_op | source)
XLA Modules:
  0.0 202.5 jit_solution(8389380161461674209)
XLA Ops:
  6.5 3.4 %stack.2 = bf16[32,2048,32]{1,2,0:T(8,128)(2,1)} broadcast(bf16[2048,32]{0,1:T(8,128)(2,1)} %param.4), dimensions={1,2} | broadcast | bytes 4325376 | tf_op jit(solution)/shard_map/stack | solution.py:21
  9.9 0.0 copy-start
  9.9 10.4 %all-to-all-start = ((bf16[32,2048,32]{1,2,0:T(8,128)(2,1)}), bf16[32,2048,32]{1,2,0:T(8,128)(2,1)}, u32[]{:S(2)}, u32[]{:S(2)}) async-start(bf16[32,2048,32]{1,2,0:T(8,128)(2,1)} %stack.2), calls=%async_computation | async-start | bytes 8388608 | tf_op jit(solution)/shard_map/all_to_all | solution.py:21
  20.3 0.0 reduce-scatter.2.cloned.1.call-start
  20.4 0.0 copy-done
  20.4 95.1 %all-to-all-done = bf16[32,2048,32]{1,2,0:T(8,128)(2,1)} async-done(((bf16[32,2048,32]{1,2,0:T(8,128)(2,1)}), bf16[32,2048,32]{1,2,0:T(8,128)(2,1)}, u32[]{:S(2)}, u32[]{:S(2)}) %all-to-all-start) | async-done | bytes 4194336 | tf_op jit(solution)/shard_map/all_to_all | solution.py:21
  115.5 0.0 copy-start.1
  115.5 0.6 mul.11
  116.1 1.6 copy-done.1
  117.7 8.6 %fusion = f32[1024,1024]{0,1:T(8,128)} fusion(bf16[2048,1024]{0,1:T(8,128)(2,1)} %bitcast.1, bf16[1024,2048]{1,0:T(8,128)(2,1)S(1)} %copy-done.1, bf16[128,8,16,128]{3,2,1,0:T(8,128)(2,1)S(1)} %bitcast.9), kind=kOutput, calls=%fused_computation.1 | convolution fusion | flops 4297064448 | bytes 16777216 | tf_op jit(solution)/shard_map/dot_general | solution.py:18
  126.2 0.0 reduce-scatter.2.cloned.1.call-update
  126.3 67.8 %reduce-scatter.2.cloned.1.call-done = f32[1024,64]{0,1:T(8,128)} async-done(((f32[1024,1024]{0,1:T(8,128)}), f32[1024,64]{0,1:T(8,128)}) %reduce-scatter.2.cloned.1.call-update) | async-done | bytes 262160 | tf_op jit(solution)/shard_map/reduce_scatter | solution.py:25
  194.1 1.6 convert_element_type.7
  (1 shorter events, 0.0 us)
Async XLA Ops:
  9.9 10.5 %copy-start = (s32[8,16]{1,0:T(8,128)S(1)}, s32[8,16]{1,0:T(8,128)}, u32[]{:S(2)}) copy-start(s32[8,16]{1,0:T(8,128)} %param.5) | copy-start | bytes 1540
  9.9 105.6 %all-to-all-start = ((bf16[32,2048,32]{1,2,0:T(8,128)(2,1)}), bf16[32,2048,32]{1,2,0:T(8,128)(2,1)}, u32[]{:S(2)}, u32[]{:S(2)}) async-start(bf16[32,2048,32]{1,2,0:T(8,128)(2,1)} %stack.2), calls=%async_computation | async-start | bytes 8388608 | tf_op jit(solution)/shard_map/all_to_all | solution.py:21
  20.3 173.7 %reduce-scatter.2.cloned.1.call-start = ((), (), s32[]{:S(2)}) async-start(), calls=%async_computation.2 | async-start | bytes 4456448 | tf_op jit(solution)/shard_map/reduce_scatter | solution.py:25
  115.5 2.2 %copy-start.1 = (bf16[1024,2048]{1,0:T(8,128)(2,1)S(1)}, bf16[1024,2048]{1,0:T(8,128)(2,1)}, u32[]{:S(2)}) copy-start(bf16[1024,2048]{1,0:T(8,128)(2,1)} %param.3) | copy-start | bytes 12582916
Sparse Core Ops, SparseCore 0:
  126.4 67.6 reduce-scatter.1
